TPU v7x, 32 devices: a whole 2x2x4 slice. The times are simulated.
32 devices in a mesh: kgrp: 4 (over x, core), band: 8 (over z, y).
Axes of the slice: x: 2, y: 2, z: 4, core: 2. Of those that a mesh axis runs over, the one named last changes fastest.
Arguments:
- densities: bfloat16 [8, 128, 128, 4096], P('kgrp', 'band'), may hold values from -6 to 6
- amplitudes: bfloat16 [8, 8, 128, 128], P('kgrp'), may hold values from -0.046875 to 0.046875
- partner: int32 [8], replicated, may hold values from 0 to 7, as said below
- qtable: int32 [8], replicated, may hold values from 0 to 63
- grid_map: int32 [64, 4096], replicated, may hold values from 0 to 4095, each once within a row
- coulomb: float32 [64, 4096], replicated, may hold values from 0.5 to 2
Outputs:
- ladder: bfloat16 [128, 8, 8, 128], P('band', 'kgrp')
Inputs may be any that keep to these rules, and one draw needn't show every extreme that they name: partner is a permutation of the 8 k-pairs; k-pair r lies in group r // 2. The two pairs of a group have their partners in two different groups, neither of them the group itself, and the two pairs whose partners lie in one group belong to two different groups. `grid_map`: each row is a permutation of the 4096 grid positions.
All inputs are finite; a program needn't handle non-finite values.
Results may differ from a plain program's by a relative error of at most 0.0064.
Values may be sent and summed in bfloat16 or wider, within the bound.
A program may use at most 448 MiB of HBM per device.

v0:
```python
import functools
import math

import jax
import jax.numpy as jnp
from jax import lax
from jax.experimental import pallas as pl
from jax.experimental.pallas import tpu as pltpu
from jax.sharding import PartitionSpec as P


def ladder_kernel(partner_ref, left_ref, right_ref, amp_ref, out_ref):
    step = pl.program_id(1)
    bands, depth, rows, width = left_ref.shape[2:]
    vb = bands * rows
    slabs = amp_ref.shape[2] // width
    left = jnp.concatenate([left_ref[0, 0, :, g].reshape(vb, width) for g in range(depth)], axis=0)
    right = jnp.concatenate([right_ref[0, 0, :, g].reshape(vb, width) for g in range(depth)], axis=1)
    mixed = jnp.dot(left, amp_ref[0], preferred_element_type=jnp.float32).astype(jnp.bfloat16)
    wide = jnp.concatenate(
        [
            jnp.concatenate(
                [mixed[g * vb:(g + 1) * vb, s * width:(s + 1) * width] for g in range(depth)], axis=1
            )
            for s in range(slabs)
        ],
        axis=0,
    )
    part = lax.dot_general(wide, right, (((1,), (1,)), ((), ())), preferred_element_type=jnp.float32)

    @pl.when(step == 0)
    def _():
        out_ref[0] = part

    @pl.when(step > 0)
    def _():
        out_ref[0] += part


def ladder_sums(blocks, amps, partner, depth):
    per_group, groups, bands, g_shard, rows, width = blocks.shape
    pairs = per_group * groups
    vb = bands * rows
    slabs = amps.shape[2] // width

    def left_map(r, s, partner_ref):
        return (lax.rem(r, per_group), r // per_group, 0, s, 0, 0)

    def right_map(r, s, partner_ref):
        q = partner_ref[r]
        return (lax.rem(q, per_group), q // per_group, 0, s, 0, 0)

    spec = (1, 1, bands, depth, rows, width)
    return pl.pallas_call(
        ladder_kernel,
        grid_spec=pltpu.PrefetchScalarGridSpec(
            num_scalar_prefetch=1,
            grid=(pairs, g_shard // depth),
            in_specs=[
                pl.BlockSpec(spec, left_map),
                pl.BlockSpec(spec, right_map),
                pl.BlockSpec((1,) + amps.shape[1:], lambda r, s, p: (r, 0, 0)),
            ],
            out_specs=pl.BlockSpec((1, slabs * vb, vb), lambda r, s, p: (r, 0, 0)),
        ),
        out_shape=jax.ShapeDtypeStruct((pairs, slabs * vb, vb), jnp.float32),
        name="ladder",
    )(partner, blocks, blocks, amps)


def shards(group_count, band_count, densities, amplitudes, partner, qtable, grid_map, coulomb):
    my_group = lax.axis_index("kgrp")
    per_group, rows, width, g_all = densities.shape
    slabs = amplitudes.shape[1]
    vb = rows * band_count
    devices = group_count * band_count
    own_ids = my_group * per_group + jnp.arange(per_group, dtype=jnp.int32)
    transfers = jnp.take(qtable, own_ids)
    positions = jnp.take(grid_map, transfers, axis=0)
    factors = jnp.take(coulomb, transfers, axis=0)
    turned = jnp.transpose(densities, (0, 3, 1, 2))
    picked = jax.vmap(lambda block, index: jnp.take(block, index, axis=0))(turned, positions)
    vertex = (picked.astype(jnp.float32) * factors[:, :, None, None]).astype(jnp.bfloat16)
    g_shard = g_all // devices
    vertex = vertex.reshape(per_group, devices, g_shard, rows, width)
    moved = lax.all_to_all(vertex, ("kgrp", "band"), split_axis=1, concat_axis=1, tiled=True)
    blocks = moved.reshape(per_group, group_count, band_count, g_shard, rows, width)
    amps = lax.all_gather(amplitudes, "kgrp", axis=0, tiled=True)
    amps = jnp.transpose(amps, (0, 2, 1, 3)).reshape(-1, width, slabs * width)
    sums = ladder_sums(blocks, amps, partner, math.gcd(g_shard, 8))
    sums = sums.reshape(-1, slabs, vb, vb)
    sums = lax.psum_scatter(sums, "kgrp", scatter_dimension=0, tiled=True)
    sums = lax.psum_scatter(sums, "band", scatter_dimension=2, tiled=True)
    scaled = sums * (1.0 / math.sqrt(g_all))
    return jnp.transpose(scaled, (2, 0, 1, 3)).astype(jnp.bfloat16)


def solution(mesh):
    in_specs = (P("kgrp", "band", None, None), P("kgrp", None, None, None), P(), P(), P(), P())
    out_specs = P("band", "kgrp", None, None)
    body = functools.partial(shards, mesh.shape["kgrp"], mesh.shape["band"])
    return jax.shard_map(body, mesh=mesh, in_specs=in_specs, out_specs=out_specs, check_vma=False)
```

profile of v0, /device:TPU:0, one launch (start us, length us, event | category | flops | bytes accessed | tf_op | source)
XLA Modules:
  0.0 1366.5 jit_solution(4326892063510615498)
XLA Ops:
  6.6 1.4 gather_fusion
  8.0 0.6 gather_fusion.1
  8.6 0.1 fusion.4
  8.7 43.3 %copy.14 = bf16[2,16,128,4096]{2,1,3,0:T(8,128)(2,1)} copy(bf16[2,16,128,4096]{3,2,1,0:T(8,128)(2,1)} %param.6) | data formatting | bytes 67108864 | tf_op args[0]
  52.0 0.1 compare_and_fusion
  52.1 1.8 gather_fusion.2
  53.9 0.1 bitcast_select_fusion
  54.0 132.8 %gather_fusion.3 = bf16[8192,16,128]{2,1,0:T(8,128)(2,1)} fusion(bf16[2,4096,16,128]{3,2,1,0:T(8,128)(2,1)} %bitcast.48, s32[8192]{0:T(1024)S(1)} %bitcast.45), kind=kCustom, calls=%fused_computation.3 | custom fusion | bytes 67174400 | tf_op jit(solution)/shard_map/vmap(jit(_take))/gather | solution.py:82
  186.8 25.2 %multiply_convert_fusion = bf16[2,32,128,16,128]{4,3,2,0,1:T(8,128)(2,1)} fusion(bf16[2,32,128,16,128]{4,3,2,1,0:T(8,128)(2,1)} %bitcast.49, f32[2,32,128]{2,0,1:T(2,128)S(1)} %copy.16, pred[2,32,128]{2,0,1:T(4,128)(4,1)S(1)} %copy.13), kind=kLoop, calls=%fused_computation.4 | loop fusion | flops 67108864 | bytes 67149824 | tf_op jit(solution)/shard_map/convert_element_type | solution.py:83
  212.0 7.5 all-to-all-start
  219.5 0.7 all-gather.2.cloned.1.call-update
  220.2 44.8 %all-gather.2.cloned.1.call-done = bf16[8,8,128,128]{3,2,1,0:T(8,128)(2,1)} async-done(((bf16[2,8,128,128]{3,2,1,0:T(8,128)(2,1)}), bf16[8,8,128,128]{3,2,1,0:T(8,128)(2,1)}) %all-gather.2.cloned.1.call-update) | async-done | bytes 2097168 | tf_op jit(solution)/shard_map/all_gather | solution.py:88
  265.0 3.2 copy_bitcast_fusion.amp_ref
  268.3 687.6 %all-to-all-done = bf16[2,32,128,16,128]{4,3,2,0,1:T(8,128)(2,1)} async-done(((bf16[2,32,128,16,128]{4,3,2,0,1:T(8,128)(2,1)}), bf16[2,32,128,16,128]{4,3,2,0,1:T(8,128)(2,1)}, u32[]{:S(2)}, u32[]{:S(2)}) %all-to-all-start) | async-done | bytes 33554464 | tf_op jit(solution)/shard_map/all_to_all | solution.py:86
  955.9 22.2 %copy.17 = bf16[2,32,128,16,128]{4,3,2,1,0:T(8,128)(2,1)} copy(bf16[2,32,128,16,128]{4,3,2,0,1:T(8,128)(2,1)} %all-to-all-done) | data formatting | bytes 67108864 | tf_op jit(solution)/shard_map/all_to_all | solution.py:86
  978.1 215.8 %ladder.1 = f32[8,1024,128]{2,1,0:T(8,128)} custom-call(s32[8]{0:T(128)} %partner_ref.1, bf16[2,4,8,128,16,128]{5,4,3,2,1,0:T(8,128)(2,1)} %bitcast.46, bf16[2,4,8,128,16,128]{5,4,3,2,1,0:T(8,128)(2,1)} %bitcast.47, bf16[8,128,1024]{2,1,0:T(8,128)(2,1)} %copy_bitcast_fusion.amp_ref), custom_call_target="tpu_custom_call" | custom-call | tf_op jit(solution)/shard_map/ladder/pallas_call | solution.py:54
  1193.9 6.7 copy.19
  1200.6 0.0 reduce-scatter.3.cloned.1.call-start
  1200.7 0.6 copy-done.2
  1201.2 0.6 dynamic-slice
  1202.5 88.1 %all-reduce.3.cloned.1.call-done = f32[8,8,128,128]{3,1,0,2:T(8,128)} async-done(((f32[8,8,128,128]{3,1,0,2:T(8,128)}), f32[8,8,128,128]{3,1,0,2:T(8,128)}) %all-reduce.3.cloned.1.call-update) | async-done | bytes 4194320
  1290.6 2.3 constant_dynamic-slice_fusion
  1292.9 65.5 %reduce-scatter.3.cloned.1.call-done = f32[2,8,16,128]{3,1,0,2:T(8,128)} async-done(((f32[2,8,128,128]{3,1,0,2:T(8,128)}), f32[2,8,16,128]{3,1,0,2:T(8,128)}) %reduce-scatter.3.cloned.1.call-update) | async-done | bytes 131088 | tf_op jit(solution)/shard_map/reduce_scatter | solution.py:93
  1358.4 1.5 fusion
  (17 shorter events, 0.2 us)
Async XLA Ops:
  6.5 1.4 copy-start
  212.0 743.9 %all-to-all-start = ((bf16[2,32,128,16,128]{4,3,2,0,1:T(8,128)(2,1)}), bf16[2,32,128,16,128]{4,3,2,0,1:T(8,128)(2,1)}, u32[]{:S(2)}, u32[]{:S(2)}) async-start(bf16[2,32,128,16,128]{4,3,2,0,1:T(8,128)(2,1)} %multiply_convert_fusion), calls=%async_computation | async-start | bytes 67108864 | tf_op jit(solution)/shard_map/all_to_all | solution.py:86
  219.5 45.6 %all-gather.2.cloned.1.call-start = ((), (), s32[]{:S(2)}) async-start(), calls=%async_computation.2 | async-start | bytes 2621440 | tf_op jit(solution)/shard_map/all_gather | solution.py:88
  220.2 1070.4 %all-reduce.3.cloned.1.call-start = ((), (), s32[]{:S(2)}) async-start(), calls=%async_computation.4 | async-start | bytes 8388608
  1193.9 166.0 %copy-start.1 = (s32[64,4096]{1,0:T(8,128)S(1)}, s32[64,4096]{1,0:T(8,128)}, u32[]{:S(2)}) copy-start(s32[64,4096]{1,0:T(8,128)} %param.10) | copy-start | bytes 3145732
  1200.6 0.7 copy-start.2
  1200.6 157.8 %reduce-scatter.3.cloned.1.call-start = ((), (), s32[]{:S(2)}) async-start(), calls=%async_computation.3 | async-start | bytes 1179648 | tf_op jit(solution)/shard_map/reduce_scatter | solution.py:93
Sparse Core Ops, SparseCore 0:
  221.8 43.1 all-gather.1
  1200.7 89.8 all-reduce.2
  1294.0 64.3 reduce-scatter.2
where the time goes:
time: 1370 us
  waiting for transfers between devices  887 us (65%)
  Pallas kernels  216 us (16%)
  local copies, waits for them, and re-layouts  215 us (16%)
  other arithmetic  27.1 us (2%)
  between operations  13.8 us (1%)
    all_to_all x1, waiting for transfers between devices, shards(): lax.all_to_all(vertex, ('kgrp', 'band'), split_axis=1, concat_axis=1, til...  688 us
    pallas_call x1, Pallas kernels, ladder_sums(): pl.pallas_call(ladder_kernel, grid_spec=pltpu.PrefetchScalarGridSpec(num_...  216 us
    gather x1, local copies, waits for them, and re-layouts, shards(): jnp.take(block, index, axis=0)  133 us
    unnamed x4, waiting for transfers between devices  88.8 us
    reduce_scatter x1, waiting for transfers between devices, shards(): sums = lax.psum_scatter(sums, 'band', scatter_dimension=2, tiled=True)  65.5 us
    unnamed x10, local copies, waits for them, and re-layouts  46.7 us
    all_gather x1, waiting for transfers between devices, shards(): amps = lax.all_gather(amplitudes, 'kgrp', axis=0, tiled=True)  44.8 us
  transfers between devices with their start and end apart: 4, of which 4 were waited for; matrix products, arithmetic and copies ran while one was open for 0% of the time, Pallas kernels for 0%

commit v1 on v0

v1 whole, which is shorter than its diff:
```python
import functools
import math

import jax
import jax.numpy as jnp
from jax import lax
from jax.experimental import pallas as pl
from jax.experimental.pallas import tpu as pltpu
from jax.sharding import PartitionSpec as P

CUTS = (1, 3, 3, 1)


def pick_kernel(index_ref, factor_ref, source_ref, out_ref):
    pair = pl.program_id(0)
    devices, _, depth = out_ref.shape[:3]

    def one(i, carry):
        d, g = i // depth, lax.rem(i, depth)
        row = source_ref[0, index_ref[pair, i]].astype(jnp.float32) * factor_ref[pair, i]
        out_ref[d, 0, g] = row.astype(out_ref.dtype)
        return carry

    lax.fori_loop(0, devices * depth, one, 0, unroll=8)


def pick_rows(turned, index, factors):
    pairs, g_all, rows, width = turned.shape
    devices, depth = index.shape[1:]
    return pl.pallas_call(
        pick_kernel,
        grid_spec=pltpu.PrefetchScalarGridSpec(
            num_scalar_prefetch=2,
            grid=(pairs,),
            in_specs=[pl.BlockSpec((1, g_all, rows, width), lambda p, i, f: (p, 0, 0, 0))],
            out_specs=pl.BlockSpec((devices, 1, depth, rows, width), lambda p, i, f: (0, p, 0, 0, 0)),
        ),
        out_shape=jax.ShapeDtypeStruct((devices, pairs, depth, rows, width), turned.dtype),
        cost_estimate=pl.CostEstimate(
            flops=pairs * devices * depth * rows * width,
            bytes_accessed=2 * turned.size + 2 * pairs * devices * depth * rows * width,
            transcendentals=0,
        ),
        compiler_params=pltpu.CompilerParams(vmem_limit_bytes=62 * 1024 * 1024),
        name="pick_rows",
    )(index.reshape(pairs, -1), factors.reshape(pairs, -1), turned)


def ladder_kernel(partner_ref, left_ref, right_ref, amp_ref, *rest):
    out_ref, total = rest[-2], rest[-1]
    step, last = pl.program_id(1), pl.num_programs(1) - 1
    bands, _, depth, rows, width = left_ref.shape[1:]
    vb = bands * rows
    slabs = amp_ref.shape[2] // width
    left = jnp.concatenate([left_ref[0, :, 0, g].reshape(vb, width) for g in range(depth)], axis=0)
    right = jnp.concatenate([right_ref[0, :, 0, g].reshape(vb, width) for g in range(depth)], axis=1)
    mixed = jnp.dot(left, amp_ref[0], preferred_element_type=jnp.float32).astype(jnp.bfloat16)
    wide = jnp.concatenate(
        [
            jnp.concatenate(
                [mixed[g * vb:(g + 1) * vb, s * width:(s + 1) * width] for g in range(depth)], axis=1
            )
            for s in range(slabs)
        ],
        axis=0,
    )
    part = lax.dot_general(wide, right, (((1,), (1,)), ((), ())), preferred_element_type=jnp.float32)

    @pl.when(step == 0)
    def _():
        total[...] = part if len(rest) == 2 else part + rest[0][0]

    @pl.when(step > 0)
    def _():
        total[...] += part

    @pl.when(step == last)
    def _():
        out_ref[0] = total[...].astype(out_ref.dtype)


def ladder_sums(blocks, amps, partner, before, kind):
    groups, bands, per_group, g_count, rows, width = blocks.shape
    pairs = per_group * groups
    vb = bands * rows
    depth = math.gcd(g_count, 8)
    slabs = amps.shape[2] // width

    def left_map(r, s, partner_ref):
        return (r // per_group, 0, lax.rem(r, per_group), s, 0, 0)

    def right_map(r, s, partner_ref):
        q = partner_ref[r]
        return (q // per_group, 0, lax.rem(q, per_group), s, 0, 0)

    spec = (1, bands, 1, depth, rows, width)
    sum_spec = pl.BlockSpec((1, slabs * vb, vb), lambda r, s, p: (r, 0, 0))
    return pl.pallas_call(
        ladder_kernel,
        grid_spec=pltpu.PrefetchScalarGridSpec(
            num_scalar_prefetch=1,
            grid=(pairs, g_count // depth),
            in_specs=[
                pl.BlockSpec(spec, left_map),
                pl.BlockSpec(spec, right_map),
                pl.BlockSpec((1,) + amps.shape[1:], lambda r, s, p: (r, 0, 0)),
            ] + [sum_spec] * len(before),
            out_specs=sum_spec,
            scratch_shapes=[pltpu.VMEM((slabs * vb, vb), jnp.float32)],
        ),
        out_shape=jax.ShapeDtypeStruct((pairs, slabs * vb, vb), kind),
        cost_estimate=pl.CostEstimate(
            flops=4 * pairs * g_count * vb * vb * vb * slabs, bytes_accessed=4 * blocks.size, transcendentals=0
        ),
        name="ladder",
    )(partner, blocks, blocks, amps, *before)


def shards(group_count, band_count, densities, amplitudes, partner, qtable, grid_map, coulomb):
    my_group = lax.axis_index("kgrp")
    per_group, rows, width, g_all = densities.shape
    slabs = amplitudes.shape[1]
    vb = rows * band_count
    devices = group_count * band_count
    g_shard = g_all // devices
    own_ids = my_group * per_group + jnp.arange(per_group, dtype=jnp.int32)
    transfers = jnp.take(qtable, own_ids)
    positions = jnp.take(grid_map, transfers, axis=0).reshape(per_group, devices, g_shard)
    factors = jnp.take(coulomb, transfers, axis=0).reshape(per_group, devices, g_shard)
    turned = jnp.transpose(densities, (0, 3, 1, 2))
    amps = lax.all_gather(amplitudes, "kgrp", axis=0, tiled=True)
    amps = jnp.transpose(amps, (0, 2, 1, 3)).reshape(-1, width, slabs * width)

    unit = sum(CUTS)
    counts = [g_shard * cut // unit for cut in CUTS] if g_shard % unit == 0 else [g_shard]
    picked, start = [], 0
    for count in counts:
        span = slice(start, start + count)
        start += count
        picked.append(pick_rows(turned, positions[:, :, span], factors[:, :, span]))
    before, moved = (), []

    def add_sums(at):
        kind = jnp.bfloat16 if at == len(counts) - 1 else jnp.float32
        return (ladder_sums(moved[at], amps, partner, before, kind),)

    for at, chunk in enumerate(picked):
        if at > 1:
            before = add_sums(at - 2)
            chunk, *before = lax.optimization_barrier((chunk, *before))
        chunk = lax.all_to_all(chunk, ("kgrp", "band"), split_axis=0, concat_axis=0, tiled=True)
        moved.append(chunk.reshape(group_count, band_count, per_group, counts[at], rows, width))
    for at in range(max(len(counts) - 2, 0), len(counts)):
        before = add_sums(at)

    sums = before[0].reshape(group_count, per_group, slabs, band_count, rows, vb)
    sums = jnp.transpose(sums, (0, 3, 1, 2, 4, 5)).reshape(devices, per_group, slabs, rows, vb)
    sums = lax.all_to_all(sums, ("kgrp", "band"), split_axis=0, concat_axis=0, tiled=True)
    summed = jnp.sum(sums.astype(jnp.float32), axis=0) * (1.0 / math.sqrt(g_all))
    return jnp.transpose(summed, (2, 0, 1, 3)).astype(jnp.bfloat16)


def solution(mesh):
    in_specs = (P("kgrp", "band", None, None), P("kgrp", None, None, None), P(), P(), P(), P())
    out_specs = P("band", "kgrp", None, None)
    body = functools.partial(shards, mesh.shape["kgrp"], mesh.shape["band"])
    return jax.shard_map(body, mesh=mesh, in_specs=in_specs, out_specs=out_specs, check_vma=False)
```

time: 1370 us -> 942 us (0.69)
  waiting for transfers between devices: 887 us -> 457 us
  local copies, waits for them, and re-layouts: 215 us -> 59.1 us
  Pallas kernels: 216 us -> 339 us
  blocking collectives: 0 us -> 51.8 us
  other arithmetic: 27.1 us -> 0.53 us
    all_to_all x1 -> x4, waiting for transfers between devices: 688 us -> 432 us  [shards(): lax.all_to_all(chunk, ('kgrp', 'band'), split_axis=0, concat_axis=0, tile...]
    gather x3 -> x2, local copies, waits for them, and re-layouts: 135 us -> 2.39 us  [the longest x1 1.82 us: shards(): jnp.take(coulomb, transfers, axis=0).reshape(per_group, devices, g_shard)]
    pallas_call x0 -> x4, Pallas kernels: none -> 113 us  [pick_rows(): pl.pallas_call(pick_kernel, grid_spec=pltpu.PrefetchScalarGridSpec(num_sc...]
    unnamed x4 -> x1, waiting for transfers between devices: 88.8 us -> 0.68 us
    reduce_scatter x1 -> x0, waiting for transfers between devices: 65.5 us -> none  [shards(): sums = lax.psum_scatter(sums, 'band', scatter_dimension=2, tiled=True)]
    all_to_all x0 -> x1, blocking collectives: none -> 51.8 us  [shards(): lax.all_to_all(sums, ('kgrp', 'band'), split_axis=0, concat_axis=0, tiled...]
    convert_element_type x2 -> x1, other arithmetic: 26.8 us -> 0.01 us  [shards(): return jnp.transpose(summed, (2, 0, 1, 3)).astype(jnp.bfloat16)]
    all_to_all x1 -> x0, local copies, waits for them, and re-layouts: 22.2 us -> none  [shards(): lax.all_to_all(vertex, ('kgrp', 'band'), split_axis=1, concat_axis=1, til...]
  transfers between devices with their start and end apart: 4 -> 5, of which waited for: 4 -> 5; matrix products, arithmetic and copies ran while one was open for 0% -> 1% of each run, Pallas kernels for 0% -> 31%
where the time goes in v1:
time: 942 us; the launch traced here: 940 us
  waiting for transfers between devices  457 us (49%)
  Pallas kernels  339 us (36%)
  local copies, waits for them, and re-layouts  59.1 us (6%)
  blocking collectives  51.8 us (5%)
  starting transfers between devices  18.6 us (2%)
  between operations  13.5 us (1%)
    all_to_all x4, waiting for transfers between devices, shards(): lax.all_to_all(chunk, ('kgrp', 'band'), split_axis=0, concat_axis=0, tile...  432 us
    pallas_call x4, Pallas kernels, ladder_sums(): pl.pallas_call(ladder_kernel, grid_spec=pltpu.PrefetchScalarGridSpec(num_...  226 us
    pallas_call x4, Pallas kernels, pick_rows(): pl.pallas_call(pick_kernel, grid_spec=pltpu.PrefetchScalarGridSpec(num_sc...  113 us
    all_to_all x1, blocking collectives, shards(): lax.all_to_all(sums, ('kgrp', 'band'), split_axis=0, concat_axis=0, tiled...  51.8 us
    unnamed x5, local copies, waits for them, and re-layouts  43.4 us
    all_gather x1, waiting for transfers between devices, shards(): amps = lax.all_gather(amplitudes, 'kgrp', axis=0, tiled=True)  24.5 us
  transfers between devices with their start and end apart: 5, of which 5 were waited for; matrix products, arithmetic and copies ran while one was open for 1% of the time, Pallas kernels for 31%

profile of v1, /device:TPU:0, one launch (start us, length us, event | category | flops | bytes accessed | tf_op | source)
XLA Modules:
  0.0 939.8 jit_solution(10796277619680359826)
XLA Ops:
  6.6 1.4 gather_fusion
  8.7 1.8 gather_fusion.2
  10.7 43.4 %copy.12 = bf16[2,16,128,4096]{2,1,3,0:T(8,128)(2,1)} copy(bf16[2,16,128,4096]{3,2,1,0:T(8,128)(2,1)} %param.6) | data formatting | bytes 67108864 | tf_op args[0]
  55.4 17.5 %pick_rows.7 = bf16[32,2,16,16,128]{4,3,2,1,0:T(8,128)(2,1)} custom-call(s32[2,512]{1,0:T(2,128)} %reshape.118.index_ref, f32[2,512]{1,0:T(2,128)} %reshape.119.factor_ref, bf16[2,4096,16,128]{3,2,1,0:T(8,128)(2,1)} %bitcast.31), custom_call_target="tpu_custom_call" | custom-call | flops 2097152 | bytes 37748736 | tf_op jit(solution)/shard_map/pick_rows/pallas_call | solution.py:30
  73.0 7.5 all-to-all-start.1
  80.5 0.7 reshape.112.index_ref
  82.0 39.0 %pick_rows.5 = bf16[32,2,48,16,128]{4,3,2,1,0:T(8,128)(2,1)} custom-call(s32[2,1536]{1,0:T(2,128)} %reshape.112.index_ref, f32[2,1536]{1,0:T(2,128)} %reshape.113.factor_ref, bf16[2,4096,16,128]{3,2,1,0:T(8,128)(2,1)} %bitcast.32), custom_call_target="tpu_custom_call" | custom-call | flops 6291456 | bytes 46137344 | tf_op jit(solution)/shard_map/pick_rows/pallas_call | solution.py:30
  121.0 55.2 %all-to-all-done.1 = bf16[32,2,16,16,128]{4,3,2,1,0:T(8,128)(2,1)} async-done(((bf16[32,2,16,16,128]{4,3,2,1,0:T(8,128)(2,1)}), bf16[32,2,16,16,128]{4,3,2,1,0:T(8,128)(2,1)}, u32[]{:S(2)}, u32[]{:S(2)}) %all-to-all-start.1) | async-done | bytes 4194336 | tf_op jit(solution)/shard_map/all_to_all | solution.py:151
  176.2 3.8 all-to-all-start
  182.1 39.0 %pick_rows.6 = bf16[32,2,48,16,128]{4,3,2,1,0:T(8,128)(2,1)} custom-call(s32[2,1536]{1,0:T(2,128)} %reshape.116.index_ref, f32[2,1536]{1,0:T(2,128)} %reshape.117.factor_ref, bf16[2,4096,16,128]{3,2,1,0:T(8,128)(2,1)} %bitcast.33), custom_call_target="tpu_custom_call" | custom-call | flops 6291456 | bytes 46137344 | tf_op jit(solution)/shard_map/pick_rows/pallas_call | solution.py:30
  221.0 24.5 %all-gather.2.cloned.1.call-done = bf16[8,8,128,128]{3,2,1,0:T(8,128)(2,1)} async-done(((bf16[2,8,128,128]{3,2,1,0:T(8,128)(2,1)}), bf16[8,8,128,128]{3,2,1,0:T(8,128)(2,1)}) %all-gather.2.cloned.1.call-update) | async-done | bytes 2097168 | tf_op jit(solution)/shard_map/all_gather | solution.py:131
  245.5 3.3 copy_bitcast_fusion.amp_ref
  248.8 29.4 %ladder.4.rest_0_ = f32[8,1024,128]{2,1,0:T(8,128)} custom-call(s32[8]{0:T(128)} %partner_ref.7, bf16[4,8,2,16,16,128]{5,4,3,2,1,0:T(8,128)(2,1)} %bitcast.6.left_ref.right_ref, bf16[4,8,2,16,16,128]{5,4,3,2,1,0:T(8,128)(2,1)} %bitcast.6.left_ref.right_ref, bf16[8,128,1024]{2,1,0:T(8,128)(2,1)} %copy_bitcast_fusion.amp_ref), custom_call_target="tpu_custom_call" | custom-call | flops 8589934592 | bytes 8388608 | tf_op jit(solution)/shard_map/ladder/pallas_call | solution.py:98
  278.2 184.3 %all-to-all-done = bf16[32,2,48,16,128]{4,3,2,1,0:T(8,128)(2,1)} async-done(((bf16[32,2,48,16,128]{4,3,2,1,0:T(8,128)(2,1)}), bf16[32,2,48,16,128]{4,3,2,1,0:T(8,128)(2,1)}, u32[]{:S(2)}, u32[]{:S(2)}) %all-to-all-start) | async-done | bytes 12582944 | tf_op jit(solution)/shard_map/all_to_all | solution.py:151
  462.6 3.8 all-to-all-start.3
  467.7 17.4 %pick_rows.4 = bf16[32,2,16,16,128]{4,3,2,1,0:T(8,128)(2,1)} custom-call(s32[2,512]{1,0:T(2,128)} %reshape.110.index_ref, f32[2,512]{1,0:T(2,128)} %reshape.111.factor_ref, bf16[2,4096,16,128]{3,2,1,0:T(8,128)(2,1)} %bitcast.34), custom_call_target="tpu_custom_call" | custom-call | flops 2097152 | bytes 37748736 | tf_op jit(solution)/shard_map/pick_rows/pallas_call | solution.py:30
  485.2 83.6 %ladder.5.rest_0_ = f32[8,1024,128]{2,1,0:T(8,128)} custom-call(s32[8]{0:T(128)} %partner_ref.7, bf16[4,8,2,48,16,128]{5,4,3,2,1,0:T(8,128)(2,1)} %bitcast.4.left_ref.right_ref, bf16[4,8,2,48,16,128]{5,4,3,2,1,0:T(8,128)(2,1)} %bitcast.4.left_ref.right_ref, bf16[8,128,1024]{2,1,0:T(8,128)(2,1)} %copy_bitcast_fusion.amp_ref, f32[8,1024,128]{2,1,0:T(8,128)} %ladder.4.rest_0_), custom_call_target="tpu_custom_call" | custom-call | flops 25769803776 | bytes 25165824 | tf_op jit(solution)/shard_map/ladder/pallas_call | solution.py:98
  568.8 180.1 %all-to-all-done.3 = bf16[32,2,48,16,128]{4,3,2,1,0:T(8,128)(2,1)} async-done(((bf16[32,2,48,16,128]{4,3,2,1,0:T(8,128)(2,1)}), bf16[32,2,48,16,128]{4,3,2,1,0:T(8,128)(2,1)}, u32[]{:S(2)}, u32[]{:S(2)}) %all-to-all-start.3) | async-done | bytes 12582944 | tf_op jit(solution)/shard_map/all_to_all | solution.py:151
  748.9 3.6 all-to-all-start.2
  752.4 83.6 %ladder.6.rest_0_ = f32[8,1024,128]{2,1,0:T(8,128)} custom-call(s32[8]{0:T(128)} %partner_ref.7, bf16[4,8,2,48,16,128]{5,4,3,2,1,0:T(8,128)(2,1)} %bitcast.8.left_ref.right_ref, bf16[4,8,2,48,16,128]{5,4,3,2,1,0:T(8,128)(2,1)} %bitcast.8.left_ref.right_ref, bf16[8,128,1024]{2,1,0:T(8,128)(2,1)} %copy_bitcast_fusion.amp_ref, f32[8,1024,128]{2,1,0:T(8,128)} %ladder.5.rest_0_), custom_call_target="tpu_custom_call" | custom-call | flops 25769803776 | bytes 25165824 | tf_op jit(solution)/shard_map/ladder/pallas_call | solution.py:98
  836.0 12.2 %all-to-all-done.2 = bf16[32,2,16,16,128]{4,3,2,1,0:T(8,128)(2,1)} async-done(((bf16[32,2,16,16,128]{4,3,2,1,0:T(8,128)(2,1)}), bf16[32,2,16,16,128]{4,3,2,1,0:T(8,128)(2,1)}, u32[]{:S(2)}, u32[]{:S(2)}) %all-to-all-start.2) | async-done | bytes 4194336 | tf_op jit(solution)/shard_map/all_to_all | solution.py:151
  848.2 29.7 %ladder.7 = bf16[8,1024,128]{2,1,0:T(8,128)(2,1)} custom-call(s32[8]{0:T(128)} %partner_ref.7, bf16[4,8,2,16,16,128]{5,4,3,2,1,0:T(8,128)(2,1)} %bitcast.7.left_ref.right_ref, bf16[4,8,2,16,16,128]{5,4,3,2,1,0:T(8,128)(2,1)} %bitcast.7.left_ref.right_ref, bf16[8,128,1024]{2,1,0:T(8,128)(2,1)} %copy_bitcast_fusion.amp_ref, f32[8,1024,128]{2,1,0:T(8,128)} %ladder.6.rest_0_), custom_call_target="tpu_custom_call" | custom-call | flops 8589934592 | bytes 8388608 | tf_op jit(solution)/shard_map/ladder/pallas_call | solution.py:98
  877.9 2.3 copy.14
  880.1 51.8 %all_to_all.25 = bf16[32,2,8,16,128]{4,3,2,1,0:T(8,128)(2,1)S(1)} all-to-all(bf16[32,2,8,16,128]{4,3,2,1,0:T(8,128)(2,1)S(1)} %bitcast.35), channel_id=1, replica_groups=mesh['kgrp'=4,'band'=8] {'kgrp','band'}, dimensions={0} | all-to-all | bytes 4194304 | tf_op jit(solution)/shard_map/all_to_all | solution.py:158
  (28 shorter events, 7.6 us)
Async XLA Ops:
  6.5 1.4 copy-start
  73.0 103.2 %all-to-all-start.1 = ((bf16[32,2,16,16,128]{4,3,2,1,0:T(8,128)(2,1)}), bf16[32,2,16,16,128]{4,3,2,1,0:T(8,128)(2,1)}, u32[]{:S(2)}, u32[]{:S(2)}) async-start(bf16[32,2,16,16,128]{4,3,2,1,0:T(8,128)(2,1)} %pick_rows.7), calls=%async_computation.1 | async-start | bytes 8388608 | tf_op jit(solution)/shard_map/all_to_all | solution.py:151
  176.2 286.4 %all-to-all-start = ((bf16[32,2,48,16,128]{4,3,2,1,0:T(8,128)(2,1)}), bf16[32,2,48,16,128]{4,3,2,1,0:T(8,128)(2,1)}, u32[]{:S(2)}, u32[]{:S(2)}) async-start(bf16[32,2,48,16,128]{4,3,2,1,0:T(8,128)(2,1)} %pick_rows.5), calls=%async_computation | async-start | bytes 25165824 | tf_op jit(solution)/shard_map/all_to_all | solution.py:151
  180.0 65.6 %all-gather.2.cloned.1.call-start = ((), (), s32[]{:S(2)}) async-start(), calls=%async_computation.5 | async-start | bytes 2621440 | tf_op jit(solution)/shard_map/all_gather | solution.py:131
  462.6 286.3 %all-to-all-start.3 = ((bf16[32,2,48,16,128]{4,3,2,1,0:T(8,128)(2,1)}), bf16[32,2,48,16,128]{4,3,2,1,0:T(8,128)(2,1)}, u32[]{:S(2)}, u32[]{:S(2)}) async-start(bf16[32,2,48,16,128]{4,3,2,1,0:T(8,128)(2,1)} %pick_rows.6), calls=%async_computation.3 | async-start | bytes 25165824 | tf_op jit(solution)/shard_map/all_to_all | solution.py:151
  748.9 99.3 %all-to-all-start.2 = ((bf16[32,2,16,16,128]{4,3,2,1,0:T(8,128)(2,1)}), bf16[32,2,16,16,128]{4,3,2,1,0:T(8,128)(2,1)}, u32[]{:S(2)}, u32[]{:S(2)}) async-start(bf16[32,2,16,16,128]{4,3,2,1,0:T(8,128)(2,1)} %pick_rows.4), calls=%async_computation.2 | async-start | bytes 8388608 | tf_op jit(solution)/shard_map/all_to_all | solution.py:151
  877.9 55.1 %copy-start.1 = (s32[64,4096]{1,0:T(8,128)S(1)}, s32[64,4096]{1,0:T(8,128)}, u32[]{:S(2)}) copy-start(s32[64,4096]{1,0:T(8,128)} %param.10) | copy-start | bytes 3145732
Sparse Core Ops, SparseCore 0:
  182.3 63.1 all-gather.1

commit v2 on v1

v2 whole, which is shorter than its diff:
```python
import functools
import math

import jax
import jax.numpy as jnp
from jax import lax
from jax.experimental import pallas as pl
from jax.experimental.pallas import tpu as pltpu
from jax.sharding import PartitionSpec as P

CUTS = (3, 8, 4, 1)


def turn_kernel(source_ref, out_ref):
    rows, width, count = source_ref.shape[1:]
    flat = source_ref[0].reshape(rows * width, count)
    out_ref[0] = flat.T.reshape(count, rows, width)


def turn(densities, pair):
    _, rows, width, g_all = densities.shape
    count = math.gcd(g_all, 256)
    moved = rows * width * g_all
    return pl.pallas_call(
        turn_kernel,
        grid=(g_all // count,),
        in_specs=[pl.BlockSpec((1, rows, width, count), lambda g: (pair, 0, 0, g))],
        out_specs=pl.BlockSpec((1, count, rows, width), lambda g: (0, g, 0, 0)),
        out_shape=jax.ShapeDtypeStruct((1, g_all, rows, width), densities.dtype),
        cost_estimate=pl.CostEstimate(flops=moved, bytes_accessed=4 * moved, transcendentals=0),
        name="turn",
    )(densities)


def pick_kernel(index_ref, factor_ref, *refs):
    *source_refs, out_ref = refs
    devices, _, depth = out_ref.shape[:3]

    def one_pair(pair, source_ref):
        def one(i, carry):
            d, g = i // depth, lax.rem(i, depth)
            row = source_ref[0, index_ref[pair, i]].astype(jnp.float32) * factor_ref[pair, i]
            out_ref[d, 0, g] = row.astype(out_ref.dtype)
            return carry

        lax.fori_loop(0, devices * depth, one, 0, unroll=8)

    for pair, source_ref in enumerate(source_refs):
        pl.when(pl.program_id(0) == pair)(functools.partial(one_pair, pair, source_ref))


def pick_rows(sources, index, factors):
    pairs = len(sources)
    _, g_all, rows, width = sources[0].shape
    devices, depth = index.shape[1:]
    moved = pairs * devices * depth * rows * width
    return pl.pallas_call(
        pick_kernel,
        grid_spec=pltpu.PrefetchScalarGridSpec(
            num_scalar_prefetch=2,
            grid=(pairs,),
            in_specs=[
                pl.BlockSpec(
                    (1, g_all, rows, width), lambda p, i, f: (0, 0, 0, 0), pipeline_mode=pl.Buffered(1)
                )
            ] * pairs,
            out_specs=pl.BlockSpec((devices, 1, depth, rows, width), lambda p, i, f: (0, p, 0, 0, 0)),
        ),
        out_shape=jax.ShapeDtypeStruct((devices, pairs, depth, rows, width), sources[0].dtype),
        cost_estimate=pl.CostEstimate(
            flops=moved, bytes_accessed=2 * pairs * sources[0].size + 2 * moved, transcendentals=0
        ),
        compiler_params=pltpu.CompilerParams(vmem_limit_bytes=62 * 1024 * 1024),
        name="pick_rows",
    )(index.reshape(pairs, -1), factors.reshape(pairs, -1), *sources)


def ladder_kernel(partner_ref, slot_ref, left_ref, right_ref, amp_ref, *rest):
    out_ref, total = rest[-2], rest[-1]
    step, last = pl.program_id(1), pl.num_programs(1) - 1
    bands, _, depth, rows, width = left_ref.shape[1:]
    vb = bands * rows
    slabs = amp_ref.shape[2] // width
    left = jnp.concatenate([left_ref[0, :, 0, g].reshape(vb, width) for g in range(depth)], axis=0)
    right = jnp.concatenate([right_ref[0, :, 0, g].reshape(vb, width) for g in range(depth)], axis=1)
    mixed = jnp.dot(left, amp_ref[0], preferred_element_type=jnp.float32).astype(jnp.bfloat16)
    wide = jnp.concatenate(
        [
            jnp.concatenate(
                [mixed[g * vb:(g + 1) * vb, s * width:(s + 1) * width] for g in range(depth)], axis=1
            )
            for s in range(slabs)
        ],
        axis=0,
    )
    part = lax.dot_general(wide, right, (((1,), (1,)), ((), ())), preferred_element_type=jnp.float32)

    @pl.when(step == 0)
    def _():
        total[...] = part if len(rest) == 2 else part + rest[0][0]

    @pl.when(step > 0)
    def _():
        total[...] += part

    @pl.when(step == last)
    def _():
        out_ref[0] = total[...].astype(out_ref.dtype)


def ladder_sums(blocks, amps, partner, slots, before, kind):
    groups, bands, per_group, g_count, rows, width = blocks.shape
    pairs = per_group * groups
    vb = bands * rows
    depth = math.gcd(g_count, 8)
    slabs = amps.shape[2] // width

    def left_map(r, s, partner_ref, slot_ref):
        return (r // per_group, 0, lax.rem(r, per_group), s, 0, 0)

    def right_map(r, s, partner_ref, slot_ref):
        q = partner_ref[r]
        return (q // per_group, 0, lax.rem(q, per_group), s, 0, 0)

    def amp_map(r, s, partner_ref, slot_ref):
        return (slot_ref[r // per_group] * per_group + lax.rem(r, per_group), 0, 0)

    spec = (1, bands, 1, depth, rows, width)
    sum_spec = pl.BlockSpec((1, slabs * vb, vb), lambda r, s, p, q: (r, 0, 0))
    return pl.pallas_call(
        ladder_kernel,
        grid_spec=pltpu.PrefetchScalarGridSpec(
            num_scalar_prefetch=2,
            grid=(pairs, g_count // depth),
            in_specs=[
                pl.BlockSpec(spec, left_map),
                pl.BlockSpec(spec, right_map),
                pl.BlockSpec((1,) + amps.shape[1:], amp_map),
            ] + [sum_spec] * len(before),
            out_specs=sum_spec,
            scratch_shapes=[pltpu.VMEM((slabs * vb, vb), jnp.float32)],
        ),
        out_shape=jax.ShapeDtypeStruct((pairs, slabs * vb, vb), kind),
        cost_estimate=pl.CostEstimate(
            flops=4 * pairs * g_count * vb * vb * vb * slabs, bytes_accessed=4 * blocks.size, transcendentals=0
        ),
        name="ladder",
    )(partner, slots, blocks, blocks, amps, *before)


def shards(group_count, band_count, densities, amplitudes, partner, qtable, grid_map, coulomb):
    my_group = lax.axis_index("kgrp")
    per_group, rows, width, g_all = densities.shape
    slabs = amplitudes.shape[1]
    vb = rows * band_count
    devices = group_count * band_count
    g_shard = g_all // devices
    own_ids = my_group * per_group + jnp.arange(per_group, dtype=jnp.int32)
    transfers = jnp.take(qtable, own_ids)
    positions = jnp.take(grid_map, transfers, axis=0).reshape(per_group, devices, g_shard)
    factors = jnp.take(coulomb, transfers, axis=0).reshape(per_group, devices, g_shard)
    held = jnp.transpose(amplitudes, (0, 2, 1, 3)).reshape(per_group, width, slabs * width)
    arrived = [held]
    for shift in range(1, group_count):
        ring = [(source, (source + shift) % group_count) for source in range(group_count)]
        arrived.append(lax.ppermute(held, "kgrp", ring))
    amps = jnp.concatenate(arrived, axis=0)
    slots = lax.rem(my_group - jnp.arange(group_count, dtype=jnp.int32) + group_count, group_count)

    unit = sum(CUTS)
    counts = [g_shard * cut // unit for cut in CUTS] if g_shard % unit == 0 else [g_shard]
    starts = [sum(counts[:at]) for at in range(len(counts))]

    def exchange(chunk):
        return lax.all_to_all(chunk, ("kgrp", "band"), split_axis=0, concat_axis=0, tiled=True)

    def pick(at, first, count):
        span = slice(starts[at], starts[at] + counts[at])
        own = slice(first, first + count)
        return pick_rows(turned[own], positions[own, :, span], factors[own, :, span])

    turned, firsts, source = [], [], densities
    for p in range(per_group):
        turned.append(turn(source, p))
        chunk = pick(0, p, 1)
        chunk, source = lax.optimization_barrier((chunk, source))
        firsts.append(exchange(chunk))
    tables = [jnp.concatenate(firsts, axis=1)]

    before = ()

    def add_sums(at):
        kind = jnp.bfloat16 if at == len(counts) - 1 else jnp.float32
        blocks = tables[at].reshape(group_count, band_count, per_group, counts[at], rows, width)
        return (ladder_sums(blocks, amps, partner, slots, before, kind),)

    for at in range(1, len(counts)):
        chunk = pick(at, 0, per_group)
        if at > 1:
            before = add_sums(at - 2)
            chunk, *before = lax.optimization_barrier((chunk, *before))
        tables.append(exchange(chunk))
    for at in range(max(len(counts) - 2, 0), len(counts)):
        before = add_sums(at)

    sums = before[0].reshape(group_count, per_group, slabs, band_count, rows, vb)
    sums = jnp.transpose(sums, (0, 3, 1, 2, 4, 5)).reshape(devices, per_group, slabs, rows, vb)
    sums = lax.all_to_all(sums, ("kgrp", "band"), split_axis=0, concat_axis=0, tiled=True)
    summed = jnp.sum(sums.astype(jnp.float32), axis=0) * (1.0 / math.sqrt(g_all))
    return jnp.transpose(summed, (2, 0, 1, 3)).astype(jnp.bfloat16)


def solution(mesh):
    in_specs = (P("kgrp", "band", None, None), P("kgrp", None, None, None), P(), P(), P(), P())
    out_specs = P("band", "kgrp", None, None)
    body = functools.partial(shards, mesh.shape["kgrp"], mesh.shape["band"])
    return jax.shard_map(body, mesh=mesh, in_specs=in_specs, out_specs=out_specs, check_vma=False)
```

time: 942 us -> 904 us (0.960)
  waiting for transfers between devices: 457 us -> 400 us
  Pallas kernels: 339 us -> 394 us
  local copies, waits for them, and re-layouts: 59.1 us -> 21.8 us
  between operations: 13.5 us -> 0.15 us
    all_to_all x4 -> x5, waiting for transfers between devices: 432 us -> 292 us  [exchange(): lax.all_to_all(chunk, ('kgrp', 'band'), split_axis=0, concat_axis=0, tile...]
    ppermute x0 -> x3, waiting for transfers between devices: none -> 107 us  [shards(): arrived.append(lax.ppermute(held, 'kgrp', ring))]
    pallas_call x0 -> x2, Pallas kernels: none -> 40.3 us  [turn(): pl.pallas_call(turn_kernel, grid=(g_all // count,), in_specs=[pl.BlockSpe...]
    unnamed x5 -> x11, local copies, waits for them, and re-layouts: 43.4 us -> 6.02 us
    all_gather x1 -> x0, waiting for transfers between devices: 24.5 us -> none  [shards(): amps = lax.all_gather(amplitudes, 'kgrp', axis=0, tiled=True)]
    pallas_call x4 -> x5, Pallas kernels: 113 us -> 128 us  [pick_rows(): pl.pallas_call(pick_kernel, grid_spec=pltpu.PrefetchScalarGridSpec(num_sc...]
    all_to_all x4 -> x5, starting transfers between devices: 18.6 us -> 21.3 us  [exchange(): lax.all_to_all(chunk, ('kgrp', 'band'), split_axis=0, concat_axis=0, tile...]
  transfers between devices with their start and end apart: 5 -> 8, of which waited for: 5 -> 7; matrix products, arithmetic and copies ran while one was open for 1% -> 2% of each run, Pallas kernels for 31% -> 38%
where the time goes in v2:
time: 904 us; the launch traced here: 902 us
  waiting for transfers between devices  400 us (44%)
  Pallas kernels  394 us (44%)
  blocking collectives  55.6 us (6%)
  starting transfers between devices  24.4 us (3%)
  local copies, waits for them, and re-layouts  21.8 us (2%)
    all_to_all x5, waiting for transfers between devices, exchange(): lax.all_to_all(chunk, ('kgrp', 'band'), split_axis=0, concat_axis=0, tile...  292 us
    pallas_call x4, Pallas kernels, ladder_sums(): pl.pallas_call(ladder_kernel, grid_spec=pltpu.PrefetchScalarGridSpec(num_...  226 us
    pallas_call x5, Pallas kernels, pick_rows(): pl.pallas_call(pick_kernel, grid_spec=pltpu.PrefetchScalarGridSpec(num_sc...  128 us
    ppermute x3, waiting for transfers between devices, shards(): arrived.append(lax.ppermute(held, 'kgrp', ring))  107 us
    all_to_all x1, blocking collectives, shards(): lax.all_to_all(sums, ('kgrp', 'band'), split_axis=0, concat_axis=0, tiled...  55.6 us
    pallas_call x2, Pallas kernels, turn(): pl.pallas_call(turn_kernel, grid=(g_all // count,), in_specs=[pl.BlockSpe...  40.3 us
    all_to_all x5, starting transfers between devices, exchange(): lax.all_to_all(chunk, ('kgrp', 'band'), split_axis=0, concat_axis=0, tile...  21.3 us
  transfers between devices with their start and end apart: 8, of which 7 were waited for; matrix products, arithmetic and copies ran while one was open for 2% of the time, Pallas kernels for 38%

profile of v2, /device:TPU:0, one launch (start us, length us, event | category | flops | bytes accessed | tf_op | source)
XLA Modules:
  0.0 902.5 jit_solution(11984950354443412854)
XLA Ops:
  5.4 20.2 %turn.2.refs_0_ = bf16[1,4096,16,128]{3,2,1,0:T(8,128)(2,1)} custom-call(bf16[2,16,128,4096]{3,2,1,0:T(8,128)(2,1)} %source_ref.2), custom_call_target="tpu_custom_call" | custom-call | flops 8388608 | bytes 33554432 | tf_op jit(solution)/shard_map/turn/pallas_call | solution.py:24
  25.5 14.3 %pick_rows.5 = bf16[32,1,24,16,128]{4,3,2,1,0:T(8,128)(2,1)} custom-call(s32[1,768]{1,0:T(1,128)} %reshape.118.index_ref, f32[1,768]{1,0:T(1,128)} %reshape.119.factor_ref, bf16[1,4096,16,128]{3,2,1,0:T(8,128)(2,1)} %turn.2.refs_0_), custom_call_target="tpu_custom_call" | custom-call | flops 1572864 | bytes 19922944 | tf_op jit(solution)/shard_map/pick_rows/pallas_call | solution.py:57
  39.8 7.4 all-to-all-start.1
  48.6 20.2 %turn.3.refs_1_.refs_0_ = bf16[1,4096,16,128]{3,2,1,0:T(8,128)(2,1)} custom-call(bf16[2,16,128,4096]{3,2,1,0:T(8,128)(2,1)} %source_ref.2), custom_call_target="tpu_custom_call" | custom-call | flops 8388608 | bytes 33554432 | tf_op jit(solution)/shard_map/turn/pallas_call | solution.py:24
  68.8 14.3 %pick_rows.9 = bf16[32,1,24,16,128]{4,3,2,1,0:T(8,128)(2,1)} custom-call(s32[1,768]{1,0:T(1,128)} %reshape.126.index_ref, f32[1,768]{1,0:T(1,128)} %reshape.127.factor_ref, bf16[1,4096,16,128]{3,2,1,0:T(8,128)(2,1)} %turn.3.refs_1_.refs_0_), custom_call_target="tpu_custom_call" | custom-call | flops 1572864 | bytes 19922944 | tf_op jit(solution)/shard_map/pick_rows/pallas_call | solution.py:57
  83.1 37.1 %all-to-all-done.1 = bf16[32,1,24,16,128]{4,3,2,1,0:T(8,128)(2,1)} async-done(((bf16[32,1,24,16,128]{4,3,2,1,0:T(8,128)(2,1)}), bf16[32,1,24,16,128]{4,3,2,1,0:T(8,128)(2,1)}, u32[]{:S(2)}, u32[]{:S(2)}) %all-to-all-start.1) | async-done | bytes 3145760 | tf_op jit(solution)/shard_map/all_to_all | solution.py:175
  120.2 3.6 all-to-all-start.2
  125.3 50.9 %pick_rows.7 = bf16[32,2,64,16,128]{4,3,2,1,0:T(8,128)(2,1)} custom-call(s32[2,2048]{1,0:T(2,128)} %reshape.120.index_ref, f32[2,2048]{1,0:T(2,128)} %reshape.121.factor_ref, bf16[1,4096,16,128]{3,2,1,0:T(8,128)(2,1)} %turn.2.refs_0_, bf16[1,4096,16,128]{3,2,1,0:T(8,128)(2,1)} %turn.3.refs_1_.refs_0_), custom_call_target="tpu_custom_call" | custom-call | flops 8388608 | bytes 50331648 | tf_op jit(solution)/shard_map/pick_rows/pallas_call | solution.py:57
  176.2 20.6 %all-to-all-done.2 = bf16[32,1,24,16,128]{4,3,2,1,0:T(8,128)(2,1)} async-done(((bf16[32,1,24,16,128]{4,3,2,1,0:T(8,128)(2,1)}), bf16[32,1,24,16,128]{4,3,2,1,0:T(8,128)(2,1)}, u32[]{:S(2)}, u32[]{:S(2)}) %all-to-all-start.2) | async-done | bytes 3145760 | tf_op jit(solution)/shard_map/all_to_all | solution.py:175
  196.8 3.9 all-to-all-start
  205.9 31.4 %pick_rows.8 = bf16[32,2,32,16,128]{4,3,2,1,0:T(8,128)(2,1)} custom-call(s32[2,1024]{1,0:T(2,128)} %reshape.124.index_ref, f32[2,1024]{1,0:T(2,128)} %reshape.125.factor_ref, bf16[1,4096,16,128]{3,2,1,0:T(8,128)(2,1)} %turn.2.refs_0_, bf16[1,4096,16,128]{3,2,1,0:T(8,128)(2,1)} %turn.3.refs_1_.refs_0_), custom_call_target="tpu_custom_call" | custom-call | flops 4194304 | bytes 41943040 | tf_op jit(solution)/shard_map/pick_rows/pallas_call | solution.py:57
  238.3 81.2 %collective-permute-done = bf16[2,128,1024]{2,1,0:T(8,128)(2,1)} collective-permute-done((bf16[2,128,1024]{2,1,0:T(8,128)(2,1)S(1)}, bf16[2,128,1024]{2,1,0:T(8,128)(2,1)}, u32[]{:S(2)}, u32[]{:S(2)}) %collective-permute-start) | collective-permute-done | bytes 524320 | tf_op jit(solution)/shard_map/ppermute | solution.py:166
  321.4 8.4 collective-permute-done.1
  331.6 17.5 %collective-permute-done.2 = bf16[2,128,1024]{2,1,0:T(8,128)(2,1)} collective-permute-done((bf16[2,128,1024]{2,1,0:T(8,128)(2,1)S(1)}, bf16[2,128,1024]{2,1,0:T(8,128)(2,1)}, u32[]{:S(2)}, u32[]{:S(2)}) %collective-permute-start.2) | collective-permute-done | bytes 524320 | tf_op jit(solution)/shard_map/ppermute | solution.py:166
  351.1 6.2 pad_maximum_fusion
  357.3 43.2 %ladder.4.rest_0_ = f32[8,1024,128]{2,1,0:T(8,128)} custom-call(s32[8]{0:T(128)} %partner_ref.7, s32[4]{0:T(128)} %compare_select_fusion.4.slot_ref, bf16[4,8,2,24,16,128]{5,4,3,2,1,0:T(8,128)(2,1)} %bitcast.35, bf16[4,8,2,24,16,128]{5,4,3,2,1,0:T(8,128)(2,1)} %bitcast.36, bf16[8,128,1024]{2,1,0:T(8,128)(2,1)} %constant_dynamic-update-slice_fusion.amp_ref), custom_call_target="tpu_custom_call" | custom-call | flops 12884901888 | bytes 12582912 | tf_op jit(solution)/shard_map/ladder/pallas_call | solution.py:130
  400.5 175.2 %all-to-all-done = bf16[32,2,64,16,128]{4,3,2,1,0:T(8,128)(2,1)} async-done(((bf16[32,2,64,16,128]{4,3,2,1,0:T(8,128)(2,1)}), bf16[32,2,64,16,128]{4,3,2,1,0:T(8,128)(2,1)}, u32[]{:S(2)}, u32[]{:S(2)}) %all-to-all-start) | async-done | bytes 16777248 | tf_op jit(solution)/shard_map/all_to_all | solution.py:175
  575.7 3.7 all-to-all-start.4
  580.9 16.8 %pick_rows.6 = bf16[32,2,8,16,128]{4,3,2,1,0:T(8,128)(2,1)} custom-call(s32[2,256]{1,0:T(2,128)} %reshape.116.index_ref, f32[2,256]{1,0:T(2,128)} %reshape.117.factor_ref, bf16[1,4096,16,128]{3,2,1,0:T(8,128)(2,1)} %turn.2.refs_0_, bf16[1,4096,16,128]{3,2,1,0:T(8,128)(2,1)} %turn.3.refs_1_.refs_0_), custom_call_target="tpu_custom_call" | custom-call | flops 1048576 | bytes 35651584 | tf_op jit(solution)/shard_map/pick_rows/pallas_call | solution.py:57
  597.7 111.7 %ladder.5.rest_0_ = f32[8,1024,128]{2,1,0:T(8,128)} custom-call(s32[8]{0:T(128)} %partner_ref.7, s32[4]{0:T(128)} %compare_select_fusion.4.slot_ref, bf16[4,8,2,64,16,128]{5,4,3,2,1,0:T(8,128)(2,1)} %bitcast.3.left_ref.right_ref, bf16[4,8,2,64,16,128]{5,4,3,2,1,0:T(8,128)(2,1)} %bitcast.3.left_ref.right_ref, ...), custom_call_target="tpu_custom_call" | custom-call | flops 34359738368 | bytes 33554432 | tf_op jit(solution)/shard_map/ladder/pallas_call | solution.py:130
  709.4 59.6 %all-to-all-done.4 = bf16[32,2,32,16,128]{4,3,2,1,0:T(8,128)(2,1)} async-done(((bf16[32,2,32,16,128]{4,3,2,1,0:T(8,128)(2,1)}), bf16[32,2,32,16,128]{4,3,2,1,0:T(8,128)(2,1)}, u32[]{:S(2)}, u32[]{:S(2)}) %all-to-all-start.4) | async-done | bytes 8388640 | tf_op jit(solution)/shard_map/all_to_all | solution.py:175
  771.7 57.3 %ladder.6.rest_0_ = f32[8,1024,128]{2,1,0:T(8,128)} custom-call(s32[8]{0:T(128)} %partner_ref.7, s32[4]{0:T(128)} %compare_select_fusion.4.slot_ref, bf16[4,8,2,32,16,128]{5,4,3,2,1,0:T(8,128)(2,1)} %bitcast.7.left_ref.right_ref, bf16[4,8,2,32,16,128]{5,4,3,2,1,0:T(8,128)(2,1)} %bitcast.7.left_ref.right_ref, ...), custom_call_target="tpu_custom_call" | custom-call | flops 17179869184 | bytes 16777216 | tf_op jit(solution)/shard_map/ladder/pallas_call | solution.py:130
  830.4 13.3 %ladder.7 = bf16[8,1024,128]{2,1,0:T(8,128)(2,1)} custom-call(s32[8]{0:T(128)} %partner_ref.7, s32[4]{0:T(128)} %compare_select_fusion.4.slot_ref, bf16[4,8,2,8,16,128]{5,4,3,2,1,0:T(8,128)(2,1)} %bitcast.37, bf16[4,8,2,8,16,128]{5,4,3,2,1,0:T(8,128)(2,1)} %bitcast.38, bf16[8,128,1024]{2,1,0:T(8,128)(2,1)} %constant_dynamic-update-slice_fusion.amp_ref, ...), custom_call_target="tpu_custom_call" | custom-call | flops 4294967296 | bytes 4194304 | tf_op jit(solution)/shard_map/ladder/pallas_call | solution.py:130
  845.9 55.6 %all_to_all.30 = bf16[32,2,8,16,128]{4,3,2,1,0:T(8,128)(2,1)S(1)} all-to-all(bf16[32,2,8,16,128]{4,3,2,1,0:T(8,128)(2,1)S(1)} %bitcast.34), channel_id=1, replica_groups=mesh['kgrp'=4,'band'=8] {'kgrp','band'}, dimensions={0} | all-to-all | bytes 4194304 | tf_op jit(solution)/shard_map/all_to_all | solution.py:208
  (51 shorter events, 28.7 us)
Async XLA Ops:
  0.0 1.4 copy-start
  39.8 80.4 %all-to-all-start.1 = ((bf16[32,1,24,16,128]{4,3,2,1,0:T(8,128)(2,1)}), bf16[32,1,24,16,128]{4,3,2,1,0:T(8,128)(2,1)}, u32[]{:S(2)}, u32[]{:S(2)}) async-start(bf16[32,1,24,16,128]{4,3,2,1,0:T(8,128)(2,1)} %pick_rows.5), calls=%async_computation.1 | async-start | bytes 6291456 | tf_op jit(solution)/shard_map/all_to_all | solution.py:175
  120.2 76.6 %all-to-all-start.2 = ((bf16[32,1,24,16,128]{4,3,2,1,0:T(8,128)(2,1)}), bf16[32,1,24,16,128]{4,3,2,1,0:T(8,128)(2,1)}, u32[]{:S(2)}, u32[]{:S(2)}) async-start(bf16[32,1,24,16,128]{4,3,2,1,0:T(8,128)(2,1)} %pick_rows.9), calls=%async_computation.2 | async-start | bytes 6291456 | tf_op jit(solution)/shard_map/all_to_all | solution.py:175
  176.2 24.5 %copy-start.3 = (bf16[2,8,128,128]{3,2,1,0:T(8,128)(2,1)S(1)}, bf16[2,8,128,128]{3,2,1,0:T(8,128)(2,1)}, u32[]{:S(2)}) copy-start(bf16[2,8,128,128]{3,2,1,0:T(8,128)(2,1)} %param.7) | copy-start | bytes 1572868
  196.8 378.9 %all-to-all-start = ((bf16[32,2,64,16,128]{4,3,2,1,0:T(8,128)(2,1)}), bf16[32,2,64,16,128]{4,3,2,1,0:T(8,128)(2,1)}, u32[]{:S(2)}, u32[]{:S(2)}) async-start(bf16[32,2,64,16,128]{4,3,2,1,0:T(8,128)(2,1)} %pick_rows.7), calls=%async_computation | async-start | bytes 33554432 | tf_op jit(solution)/shard_map/all_to_all | solution.py:175
  200.8 118.7 %collective-permute-start = (bf16[2,128,1024]{2,1,0:T(8,128)(2,1)S(1)}, bf16[2,128,1024]{2,1,0:T(8,128)(2,1)}, u32[]{:S(2)}, u32[]{:S(2)}) collective-permute-start(bf16[2,128,1024]{2,1,0:T(8,128)(2,1)S(1)} %copy_bitcast_fusion), channel_id=1, source_target_pairs={{0,8},{8,16},{16,24},{24,0},{1,9},{9,17},{17,25},{25,1},{2,10},{10... | collective-permute-start | bytes 1572872 | tf_op jit(solution)/shard_map/ppermute | solution.py:166
  200.8 128.9 %collective-permute-start.1 = (bf16[2,128,1024]{2,1,0:T(8,128)(2,1)S(1)}, bf16[2,128,1024]{2,1,0:T(8,128)(2,1)}, u32[]{:S(2)}, u32[]{:S(2)}) collective-permute-start(bf16[2,128,1024]{2,1,0:T(8,128)(2,1)S(1)} %copy_bitcast_fusion), channel_id=1, source_target_pairs={{0,16},{8,24},{16,0},{24,8},{1,17},{9,25},{17,1},{25,9},{2,18},{10... | collective-permute-start | bytes 1572872 | tf_op jit(solution)/shard_map/ppermute | solution.py:166
  202.5 146.7 %collective-permute-start.2 = (bf16[2,128,1024]{2,1,0:T(8,128)(2,1)S(1)}, bf16[2,128,1024]{2,1,0:T(8,128)(2,1)}, u32[]{:S(2)}, u32[]{:S(2)}) collective-permute-start(bf16[2,128,1024]{2,1,0:T(8,128)(2,1)S(1)} %copy_bitcast_fusion), channel_id=1, source_target_pairs={{0,24},{8,0},{16,8},{24,16},{1,25},{9,1},{17,9},{25,17},{2,26},{10... | collective-permute-start | bytes 1572872 | tf_op jit(solution)/shard_map/ppermute | solution.py:166
  575.7 193.3 %all-to-all-start.4 = ((bf16[32,2,32,16,128]{4,3,2,1,0:T(8,128)(2,1)}), bf16[32,2,32,16,128]{4,3,2,1,0:T(8,128)(2,1)}, u32[]{:S(2)}, u32[]{:S(2)}) async-start(bf16[32,2,32,16,128]{4,3,2,1,0:T(8,128)(2,1)} %pick_rows.8), calls=%async_computation.4 | async-start | bytes 16777216 | tf_op jit(solution)/shard_map/all_to_all | solution.py:175
  769.0 60.0 %all-to-all-start.3 = ((bf16[32,2,8,16,128]{4,3,2,1,0:T(8,128)(2,1)}), bf16[32,2,8,16,128]{4,3,2,1,0:T(8,128)(2,1)S(1)}, u32[]{:S(2)}, u32[]{:S(2)}) async-start(bf16[32,2,8,16,128]{4,3,2,1,0:T(8,128)(2,1)} %pick_rows.6), calls=%async_computation.3 | async-start | bytes 4194304 | tf_op jit(solution)/shard_map/all_to_all | solution.py:175
  829.0 1.4 copy-start.2
  845.9 56.6 %copy-start.1 = (f32[64,4096]{1,0:T(8,128)S(1)}, f32[64,4096]{1,0:T(8,128)}, u32[]{:S(2)}) copy-start(f32[64,4096]{1,0:T(8,128)} %param.11) | copy-start | bytes 3145732
